TPU v7x, 32 devices: a whole 2x2x4 slice. The times are simulated.
32 devices in a mesh: gx: 2 (over y), gy: 4 (over x, core), gz: 4 (over z).
Axes of the slice: x: 2, y: 2, z: 4, core: 2. Of those that a mesh axis runs over, the one named last changes fastest.
Arguments:
- fluid_state: float32 [4, 32, 64, 512], P(None, 'gx', 'gy', 'gz'), may hold values from -6 to 6
- shell_disp: float32 [3, 32768], P(None, ('gy', 'gz')), may hold values from -6 to 6
- quad_weights: float32 [32, 32, 64], P(('gx', 'gy', 'gz')), may hold values from 0.25 to 1
- quad_elements: int32 [32, 32, 64], P(('gx', 'gy', 'gz')), may hold values from 0 to 32767
- owner_cells: int32 [32, 32, 64], P(('gx', 'gy', 'gz')), may hold values from 0 to 32767
- owner_counts: int32 [32, 32], P(('gx', 'gy', 'gz')), may hold values from 0 to 64, as said below
Outputs:
- fluid_out: float32 [4, 32, 64, 512], P(None, 'gx', 'gy', 'gz')
- shell_out: float32 [3, 32768], P(None, ('gy', 'gz'))
Inputs may be any that keep to these rules, and one draw needn't show every extreme that they name: `owner_counts`: some owner has 64 live records from every sender; some owner has none from some sender.
All inputs are finite; a program needn't handle non-finite values.
Results may differ from a plain program's by a relative error of at most 0.000023.
Values sent between devices are 32-bit elements; how exact they have to be, the bound alone decides.
A program may use at most 128 MiB of HBM per device.

v0:
```python
import jax
import jax.numpy as jnp
from jax import lax
from jax.sharding import PartitionSpec as P

ITERS = 2
advection = 0.2
penalty = 0.5
relaxation = 0.05


def with_halo(cells, sides, width):
    for axis, dim in sides:
        count = lax.axis_size(axis)
        ends = count - 1
        head = lax.slice_in_dim(cells, 0, width, axis=dim)
        tail = lax.slice_in_dim(cells, cells.shape[dim] - width, cells.shape[dim], axis=dim)
        cells = jnp.concatenate(
            [
                lax.ppermute(tail, axis, [(i, (i + 1) % count) for i in range(ends)]),
                cells,
                lax.ppermute(head, axis, [((i + 1) % count, i) for i in range(ends)]),
            ],
            axis=dim,
        )
    return cells


def smooth_axis(values, axis):
    length = values.shape[axis] - 2
    lower = lax.slice_in_dim(values, 0, length, axis=axis)
    middle = lax.slice_in_dim(values, 1, length + 1, axis=axis)
    upper = lax.slice_in_dim(values, 2, length + 2, axis=axis)
    return 0.25 * lower + 0.5 * middle + 0.25 * upper


def sweep_fluid(padded):
    smoothed = smooth_axis(smooth_axis(smooth_axis(padded, 1), 2), 3)
    center = padded[:, 1:-1, 1:-1, 1:-1]
    grad_x = 0.5 * (padded[:, 2:, 1:-1, 1:-1] - padded[:, :-2, 1:-1, 1:-1])
    grad_y = 0.5 * (padded[:, 1:-1, 2:, 1:-1] - padded[:, 1:-1, :-2, 1:-1])
    grad_z = 0.5 * (padded[:, 1:-1, 1:-1, 2:] - padded[:, 1:-1, 1:-1, :-2])
    convect = center[0:1] * grad_x + center[1:2] * grad_y + center[2:3] * grad_z
    updated = smoothed - advection * convect
    pressure_grad = jnp.stack([grad_x[3], grad_y[3], grad_z[3]])
    return jnp.concatenate([updated[0:3] - advection * pressure_grad, updated[3:4]], 0)


def on_device(fluid_state, shell_disp, quad_weights, quad_elements, owner_cells, owner_counts):
    slots = quad_weights.shape[2]
    elements = quad_elements[0]
    cells_local = owner_cells[0]
    slot_index = jnp.arange(slots, dtype=jnp.int32)[None, :]
    live_mask = (slot_index < owner_counts[0][:, None]).astype(jnp.float32)
    block_shape = fluid_state.shape
    for iteration in range(ITERS):
        padded = with_halo(fluid_state, (("gx", 1), ("gy", 2), ("gz", 3)), 1)
        halfway = sweep_fluid(padded)
        all_nodes = lax.all_gather(shell_disp, ("gy", "gz"), axis=1, tiled=True)
        shell_vel = all_nodes[:, elements]
        records = jnp.concatenate([shell_vel, quad_weights[0][None]], 0)
        received = lax.all_to_all(
            records, ("gx", "gy", "gz"), split_axis=1, concat_axis=1, tiled=True
        )
        flat_vel = halfway[0:3].reshape(3, -1)
        velocity = flat_vel[:, cells_local]
        traction = penalty * received[3][None] * (velocity - received[0:3]) * live_mask[None]
        forcing = jnp.zeros_like(flat_vel).at[:, cells_local].add(traction)
        forcing = forcing.reshape(3, block_shape[1], block_shape[2], block_shape[3])
        fluid_state = jnp.concatenate([halfway[0:3] - forcing, halfway[3:4]], 0)
        returned = lax.all_to_all(
            traction, ("gx", "gy", "gz"), split_axis=1, concat_axis=1, tiled=True
        )
        node_terms = jnp.zeros((3, all_nodes.shape[1]), jnp.float32).at[:, elements].add(returned)
        partial_loads = lax.psum_scatter(node_terms, ("gy", "gz"), scatter_dimension=1, tiled=True)
        node_loads = lax.psum(partial_loads, "gx")
        shell_disp = shell_disp + relaxation * node_loads
    return (fluid_state, shell_disp)


def solution(mesh):
    return jax.shard_map(
        on_device,
        mesh=mesh,
        in_specs=(
            P(None, "gx", "gy", "gz"),
            P(None, ("gy", "gz")),
            P(("gx", "gy", "gz"), None, None),
            P(("gx", "gy", "gz"), None, None),
            P(("gx", "gy", "gz"), None, None),
            P(("gx", "gy", "gz"), None),
        ),
        out_specs=(P(None, "gx", "gy", "gz"), P(None, ("gy", "gz"))),
        check_vma=False,
    )
```

profile of v0, /device:TPU:0, one launch (start us, length us, event | category | flops | bytes accessed | tf_op | source)
XLA Modules:
  0.0 1414.3 jit_solution(13298228462873777052)
XLA Ops:
  16.1 359.1 %all_gather.6 = f32[3,32768]{0,1:T(8,128)} all-gather(f32[3,2048]{0,1:T(8,128)S(1)} %copy.153), channel_id=1, replica_groups=mesh['gx'=2,'gy'=4,'gz'=4] {'gy','gz'}, dimensions={1}, use_global_device_ids=true | all-gather | bytes 417792 | tf_op jit(solution)/shard_map/all_gather | solution.py:59
  375.3 11.2 gather_fusion
  387.7 5.4 all-to-all-start
  412.5 8.1 pad_maximum_fusion
  444.3 8.7 copy.157
  453.0 13.3 gather_fusion.1
  469.4 18.6 %scatter_custom_fusion = f32[3,32768]{0,1:T(8,128)} fusion(s32[2048]{0:T(1024)} %copy-done.35, f32[2048,3]{1,0:T(8,128)} %bitcast.86, f32[]{:T(128)} %constant.10.clone.1), kind=kCustom, calls=%fused_computation.14 | custom fusion | flops 6144 | bytes 393728 | tf_op jit(solution)/shard_map/scatter-add | solution.py:68
  488.0 10.0 copy.161
  503.5 10.1 all-to-all-start.1
  531.8 8.1 pad_maximum_fusion.1
  548.9 18.6 %scatter_custom_fusion.1 = f32[3,32768]{0,1:T(8,128)} fusion(s32[2048]{0:T(1024)} %copy-done.34, f32[2048,3]{1,0:T(8,128)} %bitcast.87, f32[]{:T(128)} %constant.10.clone.1), kind=kCustom, calls=%fused_computation.12 | custom fusion | flops 6144 | bytes 393728 | tf_op jit(solution)/shard_map/scatter-add | solution.py:74
  581.1 168.3 %reduce-scatter.3.cloned.1.call-done = f32[3,2048]{0,1:T(8,128)} async-done(((f32[3,32768]{0,1:T(8,128)}), f32[3,2048]{0,1:T(8,128)}) %reduce-scatter.3.cloned.1.call-update) | async-done | bytes 24592 | tf_op jit(solution)/shard_map/reduce_scatter | solution.py:75
  749.3 28.5 %psum.14 = f32[3,2048]{0,1:T(8,128)S(1)} all-reduce(f32[3,2048]{0,1:T(8,128)} %reduce-scatter.3.cloned.1.call-done), channel_id=1, replica_groups=mesh['gx'=2,'gy'=4,'gz'=4] {'gx'}, use_global_device_ids=true, to_apply=%region_3.0 | all-reduce | flops 6144 | bytes 49152 | tf_op jit(solution)/shard_map/psum | solution.py:76
  777.9 353.5 %all_gather.7 = f32[3,32768]{0,1:T(8,128)} all-gather(f32[3,2048]{0,1:T(8,128)S(1)} %multiply_add_fusion.1), channel_id=1, replica_groups=mesh['gx'=2,'gy'=4,'gz'=4] {'gy','gz'}, dimensions={1}, use_global_device_ids=true | all-gather | bytes 417792 | tf_op jit(solution)/shard_map/all_gather | solution.py:59
  1131.4 11.2 gather_fusion.2
  1149.1 8.7 copy.182
  1157.8 11.2 gather_fusion.3
  1171.1 5.8 all-to-all-start.3
  1177.0 7.2 all-to-all-done.3
  1185.5 18.4 %scatter_custom_fusion.3 = f32[3,32768]{0,1:T(8,128)} fusion(s32[2048]{0:T(1024)} %copy-done.34, f32[2048,3]{1,0:T(8,128)S(1)} %bitcast.85, f32[]{:T(128)} %constant.10.clone.1), kind=kCustom, calls=%fused_computation.8 | custom fusion | flops 6144 | bytes 393728 | tf_op jit(solution)/shard_map/scatter-add | solution.py:74
  1204.3 21.6 %scatter_custom_fusion.2 = f32[3,32768]{0,1:T(8,128)} fusion(s32[2048]{0:T(1024)} %copy-done.35, f32[2048,3]{1,0:T(8,128)S(1)} %bitcast.84, f32[]{:T(128)} %constant.10.clone.1), kind=kCustom, calls=%fused_computation.10 | custom fusion | flops 6144 | bytes 393728 | tf_op jit(solution)/shard_map/scatter-add | solution.py:68
  1225.9 10.3 copy.186
  1237.2 140.6 %reduce-scatter.5.cloned.1.call-done = f32[3,2048]{0,1:T(8,128)} async-done(((f32[3,32768]{0,1:T(8,128)}), f32[3,2048]{0,1:T(8,128)}) %reduce-scatter.5.cloned.1.call-update) | async-done | bytes 24592 | tf_op jit(solution)/shard_map/reduce_scatter | solution.py:75
  1377.7 28.5 %psum.15 = f32[3,2048]{0,1:T(8,128)S(1)} all-reduce(f32[3,2048]{0,1:T(8,128)} %reduce-scatter.5.cloned.1.call-done), channel_id=1, replica_groups=mesh['gx'=2,'gy'=4,'gz'=4] {'gx'}, use_global_device_ids=true, to_apply=%region_7.0 | all-reduce | flops 6144 | bytes 49152 | tf_op jit(solution)/shard_map/psum | solution.py:76
  (204 shorter events, 114.0 us)
Async XLA Ops:
  8.0 386.0 %collective-permute-start = (f32[4,1,16,128]{3,2,1,0:T(8,128)S(1)}, f32[4,1,16,128]{3,2,1,0:T(8,128)S(1)}, u32[]{:S(2)}, u32[]{:S(2)}) collective-permute-start(f32[4,1,16,128]{3,2,1,0:T(8,128)S(1)} %get-tuple-element.36), channel_id=1, source_target_pairs={{0,16},{1,17},{2,18},{3,19},{4,20},{5,21},{6,22},{7,23},{8,24},{9,... | collective-permute-start | bytes 98312 | tf_op jit(solution)/shard_map/ppermute | solution.py:20
  12.8 381.2 %collective-permute-start.1 = (f32[4,1,16,128]{3,2,1,0:T(8,128)S(1)}, f32[4,1,16,128]{3,2,1,0:T(8,128)S(1)}, u32[]{:S(2)}, u32[]{:S(2)}) collective-permute-start(f32[4,1,16,128]{3,2,1,0:T(8,128)S(1)} %get-tuple-element.35), channel_id=1, source_target_pairs={{16,0},{17,1},{18,2},{19,3},{20,4},{21,5},{22,6},{23,7},{24,8},{25... | collective-permute-start | bytes 98312 | tf_op jit(solution)/shard_map/ppermute | solution.py:22
  16.1 370.8 %copy-start.32 = (f32[1,32,64]{2,1,0:T(8,128)S(1)}, f32[1,32,64]{2,1,0:T(8,128)}, u32[]{:S(2)}) copy-start(f32[1,32,64]{2,1,0:T(8,128)} %param.8) | copy-start | bytes 24580
  16.1 377.0 %copy-start.5 = (f32[4,16,16,128]{3,2,1,0:T(8,128)S(1)}, f32[4,16,16,128]{3,2,1,0:T(8,128)}, u32[]{:S(2)}) copy-start(f32[4,16,16,128]{3,2,1,0:T(8,128)} %param.6) | copy-start | bytes 1572868
  16.1 377.7 %copy-start.36 = (s32[1,32,64]{2,1,0:T(8,128)S(1)}, s32[1,32,64]{2,1,0:T(8,128)}, u32[]{:S(2)}) copy-start(s32[1,32,64]{2,1,0:T(8,128)} %param.10) | copy-start | bytes 24580
  16.1 377.7 %copy-start.37 = (s32[1,32]{1,0:T(1,128)S(1)}, s32[1,32]{1,0:T(1,128)}, u32[]{:S(2)}) copy-start(s32[1,32]{1,0:T(1,128)} %param.11) | copy-start | bytes 388
  387.7 14.7 %all-to-all-start = ((f32[32,1,256]{2,1,0:T(1,128)}), f32[32,1,256]{2,1,0:T(1,128)S(1)}, u32[]{:S(2)}, u32[]{:S(2)}) async-start(f32[32,1,256]{2,1,0:T(1,128)} %reshape.189), calls=%async_computation | async-start | bytes 65536 | tf_op jit(solution)/shard_map/all_to_all | solution.py:62
  394.7 9.2 collective-permute-start.2
  396.9 11.2 collective-permute-start.3
  423.9 11.8 collective-permute-start.4
  428.0 9.0 collective-permute-start.5
  498.1 15.6 %collective-permute-start.6 = (f32[4,1,16,128]{3,2,1,0:T(8,128)S(1)}, f32[4,1,16,128]{3,2,1,0:T(8,128)S(1)}, u32[]{:S(2)}, u32[]{:S(2)}) collective-permute-start(f32[4,1,16,128]{3,2,1,0:T(8,128)S(1)} %get-tuple-element.30), channel_id=1, source_target_pairs={{0,16},{1,17},{2,18},{3,19},{4,20},{5,21},{6,22},{7,23},{8,24},{9,... | collective-permute-start | bytes 98312 | tf_op jit(solution)/shard_map/ppermute | solution.py:20
  501.5 12.3 collective-permute-start.7
  503.5 19.0 %all-to-all-start.1 = ((f32[32,1,192]{2,1,0:T(1,128)}), f32[32,1,192]{2,1,0:T(1,128)S(1)}, u32[]{:S(2)}, u32[]{:S(2)}) async-start(f32[32,1,192]{2,1,0:T(1,128)} %reshape.191), calls=%async_computation.1 | async-start | bytes 65536 | tf_op jit(solution)/shard_map/all_to_all | solution.py:71
  513.7 235.7 %reduce-scatter.3.cloned.1.call-start = ((), (), s32[]{:S(2)}) async-start(), calls=%async_computation.6 | async-start | bytes 17825792 | tf_op jit(solution)/shard_map/reduce_scatter | solution.py:75
  514.5 8.9 collective-permute-start.8
  516.6 11.0 collective-permute-start.9
  542.6 30.2 %collective-permute-start.10 = (f32[4,18,18,1]{2,1,3,0:T(8,128)S(1)}, f32[4,18,18,1]{2,1,3,0:T(8,128)S(1)}, u32[]{:S(2)}, u32[]{:S(2)}) collective-permute-start(f32[4,18,18,1]{2,1,3,0:T(8,128)S(1)} %get-tuple-element.22), channel_id=1, source_target_pairs={{0,1},{1,2},{2,3},{4,5},{5,6},{6,7},{8,9},{9,10},{10,11},{12,13},{... | collective-permute-start | bytes 15560 | tf_op jit(solution)/shard_map/ppermute | solution.py:20
  546.2 28.1 %collective-permute-start.11 = (f32[4,18,18,1]{2,1,3,0:T(8,128)S(1)}, f32[4,18,18,1]{2,1,3,0:T(8,128)S(1)}, u32[]{:S(2)}, u32[]{:S(2)}) collective-permute-start(f32[4,18,18,1]{2,1,3,0:T(8,128)S(1)} %get-tuple-element.23), channel_id=1, source_target_pairs={{1,0},{2,1},{3,2},{5,4},{6,5},{7,6},{9,8},{10,9},{11,10},{13,12},{... | collective-permute-start | bytes 15560 | tf_op jit(solution)/shard_map/ppermute | solution.py:22
  777.9 365.1 %copy-start.33 = (f32[1,32,64]{2,1,0:T(8,128)S(1)}, f32[1,32,64]{2,1,0:T(8,128)}, u32[]{:S(2)}) copy-start(f32[1,32,64]{2,1,0:T(8,128)} %param.8) | copy-start | bytes 24580
  777.9 371.1 %copy-start.6 = (f32[4,16,16,128]{3,2,1,0:T(8,128)S(1)}, f32[4,16,16,128]{3,2,1,0:T(8,128)}, u32[]{:S(2)}) copy-start(f32[4,16,16,128]{3,2,1,0:T(8,128)} %get-tuple-element.14) | copy-start | bytes 1572868
  1143.8 25.6 %all-to-all-start.2 = ((f32[32,1,256]{2,1,0:T(1,128)}), f32[32,1,256]{2,1,0:T(1,128)S(1)}, u32[]{:S(2)}, u32[]{:S(2)}) async-start(f32[32,1,256]{2,1,0:T(1,128)} %reshape.193), calls=%async_computation.3 | async-start | bytes 65536 | tf_op jit(solution)/shard_map/all_to_all | solution.py:62
  1171.1 13.1 all-to-all-start.3
  1176.9 200.8 %reduce-scatter.5.cloned.1.call-start = ((), (), s32[]{:S(2)}) async-start(), calls=%async_computation.7 | async-start | bytes 17825792 | tf_op jit(solution)/shard_map/reduce_scatter | solution.py:75
  (32 other events, 1260.3 us)
Sparse Core Ops, SparseCore 0:
  567.6 181.6 reduce-scatter.2
  1204.0 173.6 reduce-scatter.4
where the time goes:
time: 1420 us; the launch traced here: 1410 us
  blocking collectives  770 us (54%)
  waiting for transfers between devices  316 us (22%)
  local copies, waits for them, and re-layouts  151 us (11%)
  other arithmetic  107 us (8%)
  starting transfers between devices  55.2 us (4%)
  between operations  15.2 us (1%)
    all_gather x2, blocking collectives, on_device(): all_nodes = lax.all_gather(shell_disp, ('gy', 'gz'), axis=1, tiled=True)  713 us
    reduce_scatter x2, waiting for transfers between devices, on_device(): lax.psum_scatter(node_terms, ('gy', 'gz'), scatter_dimension=1, tiled=True)  309 us
    psum x2, blocking collectives, on_device(): node_loads = lax.psum(partial_loads, 'gx')  56.9 us
    scatter-add x2, other arithmetic, on_device(): forcing = jnp.zeros_like(flat_vel).at[:, cells_local].add(traction)  40.2 us
    scatter-add x2, other arithmetic, on_device(): jnp.zeros((3, all_nodes.shape[1]), jnp.float32).at[:, elements]  37 us
  transfers between devices with their start and end apart: 18, of which 3 were waited for; matrix products, arithmetic and copies ran while one was open for 9% of the time, Pallas kernels for 0%

commit v1 on v0

--- a/solution.py
+++ b/solution.py
@@ -56,7 +56,31 @@
     for iteration in range(ITERS):
         padded = with_halo(fluid_state, (("gx", 1), ("gy", 2), ("gz", 3)), 1)
         halfway = sweep_fluid(padded)
-        all_nodes = lax.all_gather(shell_disp, ("gy", "gz"), axis=1, tiled=True)
+        ways, here, step = (
+            lax.axis_size(("gy", "gz")),
+            lax.axis_index(("gy", "gz")),
+            shell_disp.shape[1],
+        )
+        shape = [n * ways if d == 1 else n for d, n in enumerate(shell_disp.shape)]
+        full = lax.dynamic_update_slice_in_dim(
+            jnp.zeros(shape, shell_disp.dtype), shell_disp, here * step, axis=1
+        )
+        going_up = going_down = shell_disp
+        for far in range(1, ways // 2 + 1):
+            going_up = lax.ppermute(
+                going_up, ("gy", "gz"), [(d, (d + 1) % ways) for d in range(ways)]
+            )
+            full = lax.dynamic_update_slice_in_dim(
+                full, going_up, (here - far) % ways * step, axis=1
+            )
+            if 2 * far < ways:
+                going_down = lax.ppermute(
+                    going_down, ("gy", "gz"), [(d, (d - 1) % ways) for d in range(ways)]
+                )
+                full = lax.dynamic_update_slice_in_dim(
+                    full, going_down, (here + far) % ways * step, axis=1
+                )
+        all_nodes = full
         shell_vel = all_nodes[:, elements]
         records = jnp.concatenate([shell_vel, quad_weights[0][None]], 0)
         received = lax.all_to_all(

time: 1420 us -> 845 us (0.60)
  blocking collectives: 770 us -> 57.3 us
  local copies, waits for them, and re-layouts: 151 us -> 210 us
  starting transfers between devices: 55.2 us -> 110 us
    all_gather x2 -> x0, blocking collectives: 713 us -> none  [on_device(): all_nodes = lax.all_gather(shell_disp, ('gy', 'gz'), axis=1, tiled=True)]
    ppermute x0 -> x30, starting transfers between devices: none -> 63.8 us  [the longest x14 57.2 us: on_device(): lax.ppermute(going_down, ('gy', 'gz'), [(d, (d - 1) % ways) for d in rang...]
    dynamic_update_slice x0 -> x31, local copies, waits for them, and re-layouts: none -> 35.4 us  [the longest x16 18.2 us: on_device(): lax.dynamic_update_slice_in_dim(full, going_up, (here - far) % ways * ste...]
    ppermute x0 -> x30, local copies, waits for them, and re-layouts: none -> 16.6 us  [the longest x16 9.06 us: on_device(): lax.ppermute(going_up, ('gy', 'gz'), [(d, (d + 1) % ways) for d in range(...]
  transfers between devices with their start and end apart: 18 -> 48, of which waited for: 3 -> 17; matrix products, arithmetic and copies ran while one was open for 9% -> 26% of each run, Pallas kernels for 0% -> 0%
where the time goes in v1:
time: 845 us; the launch traced here: 835 us
  waiting for transfers between devices  327 us (39%)
  local copies, waits for them, and re-layouts  210 us (25%)
  other arithmetic  115 us (14%)
  starting transfers between devices  110 us (13%)
  blocking collectives  57.3 us (7%)
  between operations  15.3 us (2%)
    reduce_scatter x2, waiting for transfers between devices, on_device(): lax.psum_scatter(node_terms, ('gy', 'gz'), scatter_dimension=1, tiled=True)  308 us
    psum x2, blocking collectives, on_device(): node_loads = lax.psum(partial_loads, 'gx')  57.3 us
    ppermute x14, starting transfers between devices, on_device(): lax.ppermute(going_down, ('gy', 'gz'), [(d, (d - 1) % ways) for d in rang...  57.2 us
    scatter-add x2, other arithmetic, on_device(): forcing = jnp.zeros_like(flat_vel).at[:, cells_local].add(traction)  40 us
    scatter-add x2, other arithmetic, on_device(): jnp.zeros((3, all_nodes.shape[1]), jnp.float32).at[:, elements]  37.1 us
    gather x4, local copies, waits for them, and re-layouts, on_device(): velocity = flat_vel[:, cells_local]  23.2 us
    gather x4, local copies, waits for them, and re-layouts, on_device(): shell_vel = all_nodes[:, elements]  23.2 us
    concatenate x5, other arithmetic, with_halo(): jnp.concatenate([lax.ppermute(tail, axis, [(i, (i + 1) % count) for i in...  20.4 us
  transfers between devices with their start and end apart: 48, of which 17 were waited for; matrix products, arithmetic and copies ran while one was open for 26% of the time, Pallas kernels for 0%

profile of v1, /device:TPU:0, one launch (start us, length us, event | category | flops | bytes accessed | tf_op | source)
XLA Modules:
  0.0 834.6 jit_solution(13883432602989787862)
XLA Ops:
  24.5 6.0 broadcast.119.clone
  63.3 8.1 pad_maximum_fusion
  139.7 11.2 %gather_fusion = f32[2048,3]{1,0:T(8,128)S(1)} fusion(f32[3,32768]{0,1:T(8,128)} %constant_dynamic-update-slice_fusion.16, s32[2048]{0:T(1024)S(1)} %broadcast_clamp_fusion.1), kind=kCustom, calls=%fused_computation | custom fusion | bytes 57344 | tf_op jit(solution)/shard_map/gather | solution.py:84
  152.1 6.8 all-to-all-start
  159.0 8.7 %copy.272 = f32[3,16,16,128]{0,3,2,1:T(8,128)} copy(f32[3,16,16,128]{3,2,1,0:T(8,128)S(1)} %slice_subtract_fusion.1) | data formatting | bytes 786432 | tf_op jit(solution)/shard_map/sub | solution.py:46
  167.7 11.2 %gather_fusion.1 = f32[2048,3]{1,0:T(8,128)S(1)} fusion(f32[3,32768]{0,1:T(8,128)} %bitcast.79, s32[2048]{0:T(1024)S(1)} %broadcast_clamp_fusion), kind=kCustom, calls=%fused_computation.1 | custom fusion | bytes 57344 | tf_op jit(solution)/shard_map/gather | solution.py:90
  181.1 18.4 %scatter_custom_fusion = f32[3,32768]{0,1:T(8,128)} fusion(s32[2048]{0:T(1024)} %copy-done.16, f32[2048,3]{1,0:T(8,128)S(1)} %bitcast.86, f32[]{:T(128)} %constant.136.clone.1), kind=kCustom, calls=%fused_computation.14 | custom fusion | flops 6144 | bytes 393728 | tf_op jit(solution)/shard_map/scatter-add | solution.py:92
  199.5 10.0 %copy.276 = f32[3,16,16,128]{3,2,1,0:T(8,128)S(1)} copy(f32[3,16,16,128]{0,3,2,1:T(8,128)} %bitcast.77) | data formatting | bytes 786432 | tf_op jit(solution)/shard_map/reshape | solution.py:93
  215.3 6.7 all-to-all-start.1
  240.6 8.1 pad_maximum_fusion.1
  257.7 18.6 %scatter_custom_fusion.1 = f32[3,32768]{0,1:T(8,128)} fusion(s32[2048]{0:T(1024)} %copy-done.17, f32[2048,3]{1,0:T(8,128)} %bitcast.87, f32[]{:T(128)} %constant.136.clone.1), kind=kCustom, calls=%fused_computation.12 | custom fusion | flops 6144 | bytes 393728 | tf_op jit(solution)/shard_map/scatter-add | solution.py:98
  290.4 167.7 %reduce-scatter.3.cloned.1.call-done = f32[3,2048]{0,1:T(8,128)} async-done(((f32[3,32768]{0,1:T(8,128)}), f32[3,2048]{0,1:T(8,128)}) %reduce-scatter.3.cloned.1.call-update) | async-done | bytes 24592 | tf_op jit(solution)/shard_map/reduce_scatter | solution.py:99
  458.1 28.9 %psum.14 = f32[3,2048]{0,1:T(8,128)S(1)} all-reduce(f32[3,2048]{0,1:T(8,128)} %reduce-scatter.3.cloned.1.call-done), channel_id=1, replica_groups=mesh['gx'=2,'gy'=4,'gz'=4] {'gx'}, use_global_device_ids=true, to_apply=%region_3.4 | all-reduce | flops 6144 | bytes 49152 | tf_op jit(solution)/shard_map/psum | solution.py:100
  487.0 6.0 broadcast.119
  554.3 11.2 %gather_fusion.2 = f32[2048,3]{1,0:T(8,128)S(1)} fusion(f32[3,32768]{0,1:T(8,128)} %constant_dynamic-update-slice_fusion, s32[2048]{0:T(1024)S(1)} %broadcast_clamp_fusion.1), kind=kCustom, calls=%fused_computation.2 | custom fusion | bytes 57344 | tf_op jit(solution)/shard_map/gather | solution.py:84
  569.4 8.7 %copy.314 = f32[3,16,16,128]{0,3,2,1:T(8,128)} copy(f32[3,16,16,128]{3,2,1,0:T(8,128)S(1)} %slice_subtract_fusion) | data formatting | bytes 786432 | tf_op jit(solution)/shard_map/sub | solution.py:46
  578.0 11.2 %gather_fusion.3 = f32[2048,3]{1,0:T(8,128)S(1)} fusion(f32[3,32768]{0,1:T(8,128)} %bitcast.78, s32[2048]{0:T(1024)S(1)} %broadcast_clamp_fusion), kind=kCustom, calls=%fused_computation.3 | custom fusion | bytes 57344 | tf_op jit(solution)/shard_map/gather | solution.py:90
  591.3 5.8 all-to-all-start.3
  597.2 7.2 all-to-all-done.3
  605.6 18.5 %scatter_custom_fusion.3 = f32[3,32768]{0,1:T(8,128)} fusion(s32[2048]{0:T(1024)} %copy-done.17, f32[2048,3]{1,0:T(8,128)S(1)} %bitcast.85, f32[]{:T(128)} %constant.136.clone.1), kind=kCustom, calls=%fused_computation.8 | custom fusion | flops 6144 | bytes 393728 | tf_op jit(solution)/shard_map/scatter-add | solution.py:98
  624.6 21.6 %scatter_custom_fusion.2 = f32[3,32768]{0,1:T(8,128)} fusion(s32[2048]{0:T(1024)} %copy-done.16, f32[2048,3]{1,0:T(8,128)S(1)} %bitcast.84, f32[]{:T(128)} %constant.136.clone.1), kind=kCustom, calls=%fused_computation.10 | custom fusion | flops 6144 | bytes 393728 | tf_op jit(solution)/shard_map/scatter-add | solution.py:92
  646.3 10.3 %copy.318 = f32[3,16,16,128]{3,2,1,0:T(8,128)S(1)} copy(f32[3,16,16,128]{0,3,2,1:T(8,128)} %bitcast.76) | data formatting | bytes 786432 | tf_op jit(solution)/shard_map/reshape | solution.py:93
  657.5 140.6 %reduce-scatter.5.cloned.1.call-done = f32[3,2048]{0,1:T(8,128)} async-done(((f32[3,32768]{0,1:T(8,128)}), f32[3,2048]{0,1:T(8,128)}) %reduce-scatter.5.cloned.1.call-update) | async-done | bytes 24592 | tf_op jit(solution)/shard_map/reduce_scatter | solution.py:99
  798.1 28.5 %psum.15 = f32[3,2048]{0,1:T(8,128)S(1)} all-reduce(f32[3,2048]{0,1:T(8,128)} %reduce-scatter.5.cloned.1.call-done), channel_id=1, replica_groups=mesh['gx'=2,'gy'=4,'gz'=4] {'gx'}, use_global_device_ids=true, to_apply=%region_7.8 | all-reduce | flops 6144 | bytes 49152 | tf_op jit(solution)/shard_map/psum | solution.py:100
  (286 shorter events, 239.2 us)
Async XLA Ops:
  7.2 24.4 %collective-permute-start.6 = (f32[3,2048]{1,0:T(4,128)}, f32[3,2048]{1,0:T(4,128)S(1)}, u32[]{:S(2)}, u32[]{:S(2)}) collective-permute-start(f32[3,2048]{1,0:T(4,128)} %param.7), channel_id=1, source_target_pairs={{0,1},{1,2},{2,3},{3,4},{4,5},{5,6},{6,7},{7,8},{8,9},{9,10},{10,1... | collective-permute-start | bytes 73736 | tf_op jit(solution)/shard_map/ppermute | solution.py:70
  10.3 22.7 %collective-permute-start.7 = (f32[3,2048]{1,0:T(4,128)}, f32[3,2048]{1,0:T(4,128)S(1)}, u32[]{:S(2)}, u32[]{:S(2)}) collective-permute-start(f32[3,2048]{1,0:T(4,128)} %param.7), channel_id=1, source_target_pairs={{0,15},{1,0},{2,1},{3,2},{4,3},{5,4},{6,5},{7,6},{8,7},{9,8},{10,9... | collective-permute-start | bytes 73736 | tf_op jit(solution)/shard_map/ppermute | solution.py:77
  13.5 25.4 %collective-permute-start = (f32[4,1,16,128]{3,2,1,0:T(8,128)S(1)}, f32[4,1,16,128]{3,2,1,0:T(8,128)S(1)}, u32[]{:S(2)}, u32[]{:S(2)}) collective-permute-start(f32[4,1,16,128]{3,2,1,0:T(8,128)S(1)} %get-tuple-element.38), channel_id=1, source_target_pairs={{0,16},{1,17},{2,18},{3,19},{4,20},{5,21},{6,22},{7,23},{8,24},{9,... | collective-permute-start | bytes 98312 | tf_op jit(solution)/shard_map/ppermute | solution.py:20
  17.4 21.6 %collective-permute-start.1 = (f32[4,1,16,128]{3,2,1,0:T(8,128)S(1)}, f32[4,1,16,128]{3,2,1,0:T(8,128)S(1)}, u32[]{:S(2)}, u32[]{:S(2)}) collective-permute-start(f32[4,1,16,128]{3,2,1,0:T(8,128)S(1)} %get-tuple-element.37), channel_id=1, source_target_pairs={{16,0},{17,1},{18,2},{19,3},{20,4},{21,5},{22,6},{23,7},{24,8},{25... | collective-permute-start | bytes 98312 | tf_op jit(solution)/shard_map/ppermute | solution.py:22
  34.4 12.5 %collective-permute-start.8 = (f32[3,2048]{1,0:T(4,128)S(1)}, f32[3,2048]{1,0:T(4,128)}, u32[]{:S(2)}, u32[]{:S(2)}) collective-permute-start(f32[3,2048]{1,0:T(4,128)S(1)} %collective-permute-done.6), channel_id=1, source_target_pairs={{0,1},{1,2},{2,3},{3,4},{4,5},{5,6},{6,7},{7,8},{8,9},{9,10},{10,1... | collective-permute-start | bytes 73736 | tf_op jit(solution)/shard_map/ppermute | solution.py:70
  34.4 14.7 %collective-permute-start.9 = (f32[3,2048]{1,0:T(4,128)S(1)}, f32[3,2048]{1,0:T(4,128)S(1)}, u32[]{:S(2)}, u32[]{:S(2)}) collective-permute-start(f32[3,2048]{1,0:T(4,128)S(1)} %collective-permute-done.7), channel_id=1, source_target_pairs={{0,15},{1,0},{2,1},{3,2},{4,3},{5,4},{6,5},{7,6},{8,7},{9,8},{10,9... | collective-permute-start | bytes 73736 | tf_op jit(solution)/shard_map/ppermute | solution.py:77
  44.3 10.7 %collective-permute-start.2 = (f32[4,18,1,128]{3,1,2,0:T(8,128)S(1)}, f32[4,18,1,128]{3,1,2,0:T(8,128)S(1)}, u32[]{:S(2)}, u32[]{:S(2)}) collective-permute-start(f32[4,18,1,128]{3,1,2,0:T(8,128)S(1)} %copy.330), channel_id=1, source_target_pairs={{0,4},{4,8},{8,12},{1,5},{5,9},{9,13},{2,6},{6,10},{10,14},{3,7},{... | collective-permute-start | bytes 110600 | tf_op jit(solution)/shard_map/ppermute | solution.py:20
  45.6 13.5 %collective-permute-start.3 = (f32[4,18,1,128]{3,1,2,0:T(8,128)S(1)}, f32[4,18,1,128]{3,1,2,0:T(8,128)S(1)}, u32[]{:S(2)}, u32[]{:S(2)}) collective-permute-start(f32[4,18,1,128]{3,1,2,0:T(8,128)S(1)} %copy.331), channel_id=1, source_target_pairs={{4,0},{8,4},{12,8},{5,1},{9,5},{13,9},{6,2},{10,6},{14,10},{7,3},{... | collective-permute-start | bytes 110600 | tf_op jit(solution)/shard_map/ppermute | solution.py:22
  50.5 33.3 %collective-permute-start.10 = (f32[3,2048]{1,0:T(4,128)}, f32[3,2048]{1,0:T(4,128)}, u32[]{:S(2)}, u32[]{:S(2)}) collective-permute-start(f32[3,2048]{1,0:T(4,128)} %collective-permute-done.8), channel_id=1, source_target_pairs={{0,1},{1,2},{2,3},{3,4},{4,5},{5,6},{6,7},{7,8},{8,9},{9,10},{10,1... | collective-permute-start | bytes 73736 | tf_op jit(solution)/shard_map/ppermute | solution.py:70
  50.5 37.7 %collective-permute-start.11 = (f32[3,2048]{1,0:T(4,128)S(1)}, f32[3,2048]{1,0:T(4,128)}, u32[]{:S(2)}, u32[]{:S(2)}) collective-permute-start(f32[3,2048]{1,0:T(4,128)S(1)} %collective-permute-done.9), channel_id=1, source_target_pairs={{0,15},{1,0},{2,1},{3,2},{4,3},{5,4},{6,5},{7,6},{8,7},{9,8},{10,9... | collective-permute-start | bytes 73736 | tf_op jit(solution)/shard_map/ppermute | solution.py:77
  79.3 17.7 %collective-permute-start.4 = (f32[4,18,18,1]{2,1,3,0:T(8,128)S(1)}, f32[4,18,18,1]{2,1,3,0:T(8,128)}, u32[]{:S(2)}, u32[]{:S(2)}) collective-permute-start(f32[4,18,18,1]{2,1,3,0:T(8,128)S(1)} %get-tuple-element.26), channel_id=1, source_target_pairs={{0,1},{1,2},{2,3},{4,5},{5,6},{6,7},{8,9},{9,10},{10,11},{12,13},{... | collective-permute-start | bytes 15560 | tf_op jit(solution)/shard_map/ppermute | solution.py:20
  81.2 17.2 %collective-permute-start.5 = (f32[4,18,18,1]{2,1,3,0:T(8,128)}, f32[4,18,18,1]{2,1,3,0:T(8,128)}, u32[]{:S(2)}, u32[]{:S(2)}) collective-permute-start(f32[4,18,18,1]{2,1,3,0:T(8,128)} %get-tuple-element.27), channel_id=1, source_target_pairs={{1,0},{2,1},{3,2},{5,4},{6,5},{7,6},{9,8},{10,9},{11,10},{13,12},{... | collective-permute-start | bytes 15560 | tf_op jit(solution)/shard_map/ppermute | solution.py:22
  92.6 13.8 %collective-permute-start.12 = (f32[3,2048]{1,0:T(4,128)}, f32[3,2048]{1,0:T(4,128)}, u32[]{:S(2)}, u32[]{:S(2)}) collective-permute-start(f32[3,2048]{1,0:T(4,128)} %collective-permute-done.10), channel_id=1, source_target_pairs={{0,1},{1,2},{2,3},{3,4},{4,5},{5,6},{6,7},{7,8},{8,9},{9,10},{10,1... | collective-permute-start | bytes 73736 | tf_op jit(solution)/shard_map/ppermute | solution.py:70
  95.3 13.7 %collective-permute-start.13 = (f32[3,2048]{1,0:T(4,128)}, f32[3,2048]{1,0:T(4,128)}, u32[]{:S(2)}, u32[]{:S(2)}) collective-permute-start(f32[3,2048]{1,0:T(4,128)} %collective-permute-done.11), channel_id=1, source_target_pairs={{0,15},{1,0},{2,1},{3,2},{4,3},{5,4},{6,5},{7,6},{8,7},{9,8},{10,9... | collective-permute-start | bytes 73736 | tf_op jit(solution)/shard_map/ppermute | solution.py:77
  152.1 27.2 %all-to-all-start = ((f32[32,1,256]{2,1,0:T(1,128)}), f32[32,1,256]{2,1,0:T(1,128)S(1)}, u32[]{:S(2)}, u32[]{:S(2)}) async-start(f32[32,1,256]{2,1,0:T(1,128)} %reshape.189), calls=%async_computation | async-start | bytes 65536 | tf_op jit(solution)/shard_map/all_to_all | solution.py:86
  209.6 12.5 %collective-permute-start.21 = (f32[4,1,16,128]{3,2,1,0:T(8,128)S(1)}, f32[4,1,16,128]{3,2,1,0:T(8,128)S(1)}, u32[]{:S(2)}, u32[]{:S(2)}) collective-permute-start(f32[4,1,16,128]{3,2,1,0:T(8,128)S(1)} %get-tuple-element.32), channel_id=1, source_target_pairs={{0,16},{1,17},{2,18},{3,19},{4,20},{5,21},{6,22},{7,23},{8,24},{9,... | collective-permute-start | bytes 98312 | tf_op jit(solution)/shard_map/ppermute | solution.py:20
  215.3 16.1 %all-to-all-start.1 = ((f32[32,1,192]{2,1,0:T(1,128)}), f32[32,1,192]{2,1,0:T(1,128)S(1)}, u32[]{:S(2)}, u32[]{:S(2)}) async-start(f32[32,1,192]{2,1,0:T(1,128)} %reshape.191), calls=%async_computation.1 | async-start | bytes 65536 | tf_op jit(solution)/shard_map/all_to_all | solution.py:95
  222.0 236.1 %reduce-scatter.3.cloned.1.call-start = ((), (), s32[]{:S(2)}) async-start(), calls=%async_computation.6 | async-start | bytes 17825792 | tf_op jit(solution)/shard_map/reduce_scatter | solution.py:99
  225.6 10.8 %collective-permute-start.24 = (f32[4,18,1,128]{3,1,2,0:T(8,128)S(1)}, f32[4,18,1,128]{3,1,2,0:T(8,128)S(1)}, u32[]{:S(2)}, u32[]{:S(2)}) collective-permute-start(f32[4,18,1,128]{3,1,2,0:T(8,128)S(1)} %copy.334), channel_id=1, source_target_pairs={{4,0},{8,4},{12,8},{5,1},{9,5},{13,9},{6,2},{10,6},{14,10},{7,3},{... | collective-permute-start | bytes 110600 | tf_op jit(solution)/shard_map/ppermute | solution.py:22
  251.4 30.2 %collective-permute-start.25 = (f32[4,18,18,1]{2,1,3,0:T(8,128)S(1)}, f32[4,18,18,1]{2,1,3,0:T(8,128)S(1)}, u32[]{:S(2)}, u32[]{:S(2)}) collective-permute-start(f32[4,18,18,1]{2,1,3,0:T(8,128)S(1)} %get-tuple-element.24), channel_id=1, source_target_pairs={{0,1},{1,2},{2,3},{4,5},{5,6},{6,7},{8,9},{9,10},{10,11},{12,13},{... | collective-permute-start | bytes 15560 | tf_op jit(solution)/shard_map/ppermute | solution.py:20
  255.0 28.1 %collective-permute-start.26 = (f32[4,18,18,1]{2,1,3,0:T(8,128)S(1)}, f32[4,18,18,1]{2,1,3,0:T(8,128)S(1)}, u32[]{:S(2)}, u32[]{:S(2)}) collective-permute-start(f32[4,18,18,1]{2,1,3,0:T(8,128)S(1)} %get-tuple-element.25), channel_id=1, source_target_pairs={{1,0},{2,1},{3,2},{5,4},{6,5},{7,6},{9,8},{10,9},{11,10},{13,12},{... | collective-permute-start | bytes 15560 | tf_op jit(solution)/shard_map/ppermute | solution.py:22
  566.7 22.9 %all-to-all-start.2 = ((f32[32,1,256]{2,1,0:T(1,128)}), f32[32,1,256]{2,1,0:T(1,128)S(1)}, u32[]{:S(2)}, u32[]{:S(2)}) async-start(f32[32,1,256]{2,1,0:T(1,128)} %reshape.193), calls=%async_computation.3 | async-start | bytes 65536 | tf_op jit(solution)/shard_map/all_to_all | solution.py:86
  591.3 13.1 %all-to-all-start.3 = ((f32[32,1,192]{2,1,0:T(1,128)}), f32[32,1,192]{2,1,0:T(1,128)S(1)}, u32[]{:S(2)}, u32[]{:S(2)}) async-start(f32[32,1,192]{2,1,0:T(1,128)} %reshape.195), calls=%async_computation.4 | async-start | bytes 65536 | tf_op jit(solution)/shard_map/all_to_all | solution.py:95
  597.1 200.9 %reduce-scatter.5.cloned.1.call-start = ((), (), s32[]{:S(2)}) async-start(), calls=%async_computation.7 | async-start | bytes 17825792 | tf_op jit(solution)/shard_map/reduce_scatter | solution.py:99
  (42 other events, 492.4 us)
Sparse Core Ops, SparseCore 0:
  276.4 181.6 reduce-scatter.2
  624.3 173.6 reduce-scatter.4
